TPU v7x, 128 devices: a whole 4x4x4 slice. The times are simulated.
128 devices in a mesh: tm: 16 (over x_hi, y, core), height: 8 (over x_lo, z).
Axes of the slice: x: 4 (x_hi: 2, x_lo: 2; x = x_hi * 2 + x_lo), y: 4, z: 4, core: 2. Of those that a mesh axis runs over, the one named last changes fastest.
Arguments:
- tokens: bfloat16 [32, 32, 80, 3072], P('tm', 'height'), may hold values from -6 to 6
- mod_scale: float32 [3072], replicated, may hold values from -3 to 3
- mod_shift: float32 [3072], replicated, may hold values from -3 to 3
- w_qkv: bfloat16 [3072, 4608], P(('tm', 'height')), may hold values from -0.109375 to 0.109375
- q_gain: float32 [128], replicated, may hold values from 0.25 to 1.75
- k_gain: float32 [128], replicated, may hold values from 0.25 to 1.75
- window: int32 [12, 3], replicated, may hold values from 0 to 2, as said below
- valid: int32 [32, 32, 80], replicated, may hold values from 0 to 1, as said below
Outputs:
- attended: bfloat16 [32, 32, 80, 1536], P('tm', 'height')
Inputs may be any that keep to these rules, and one draw needn't show every extreme that they name: `window`: column 0 is at most 1, column 1 at most 1, column 2 at most 2; some head has all three at these most values. `valid`: the last frames, rows and columns of the grid may be padding with 0; scattered tokens elsewhere are 0 too.
All inputs are finite; a program needn't handle non-finite values.
Results may differ from a plain program's by a relative error of at most 0.0055.
Values may be sent and summed in bfloat16 or wider, within the bound.
A program may use at most 128 MiB of HBM per device.

v0:
```python
import jax
import jax.numpy as jnp
from jax import lax
from jax.sharding import PartitionSpec as P

HDIM = 128
HEADS = 12
TT = 1
TH = 2
TW = 8
EPS = 1e-06


def with_halo(cells, sides, width):
    for axis, dim in sides:
        count = lax.axis_size(axis)
        ends = count - 1
        head = lax.slice_in_dim(cells, 0, width, axis=dim)
        tail = lax.slice_in_dim(cells, cells.shape[dim] - width, cells.shape[dim], axis=dim)
        cells = jnp.concatenate(
            [
                lax.ppermute(tail, axis, [(i, (i + 1) % count) for i in range(ends)]),
                cells,
                lax.ppermute(head, axis, [((i + 1) % count, i) for i in range(ends)]),
            ],
            axis=dim,
        )
    return cells


def modulate(tokens, mod_scale, mod_shift):
    values = tokens.astype(jnp.float32)
    mean = jnp.mean(values, axis=-1, keepdims=True)
    centred = values - mean
    variance = jnp.mean(centred * centred, axis=-1, keepdims=True)
    normed = centred * lax.rsqrt(variance + EPS)
    return (normed * (1.0 + mod_scale) + mod_shift).astype(jnp.bfloat16)


def head_norm(values, gain):
    power = jnp.mean(values * values, axis=-1, keepdims=True)
    return (values * lax.rsqrt(power + EPS) * gain).astype(jnp.bfloat16)


def tile_coords(frames, rows, width):
    shape = (frames.shape[0], rows.shape[0], width)
    columns = jnp.arange(width, dtype=jnp.int32)
    frame_tiles = jnp.broadcast_to((frames // TT)[:, None, None], shape).reshape(-1)
    row_tiles = jnp.broadcast_to((rows // TH)[None, :, None], shape).reshape(-1)
    column_tiles = jnp.broadcast_to((columns // TW)[None, None, :], shape).reshape(-1)
    return (frame_tiles, row_tiles, column_tiles)


def per_device(tokens, mod_scale, mod_shift, w_qkv, q_gain, k_gain, window, valid):
    frame_count, row_count, width, features = tokens.shape
    token_count = frame_count * row_count * width
    modulated = modulate(tokens.reshape(token_count, features), mod_scale, mod_shift)
    full_weight = lax.all_gather(w_qkv, ("tm", "height"), axis=0, tiled=True)
    qkv = jnp.dot(modulated, full_weight, preferred_element_type=jnp.float32)
    inner = qkv.shape[1] // 3
    query = head_norm(qkv[:, :inner].reshape(token_count, HEADS, HDIM), q_gain)
    key = head_norm(qkv[:, inner : 2 * inner].reshape(token_count, HEADS, HDIM), k_gain)
    value = qkv[:, 2 * inner :].astype(jnp.bfloat16)
    tiled = (frame_count // TT, TT, row_count // TH, TH, width, inner)
    stacked = jnp.stack([key.reshape(tiled), value.reshape(tiled)])
    extended = with_halo(stacked, (("tm", 1), ("height", 3)), 1)
    frames_ext = frame_count + 2 * TT
    rows_ext = row_count + 2 * TH
    key_count = frames_ext * rows_ext * width
    extended = extended.reshape(2, key_count, HEADS, HDIM)
    key_heads = jnp.transpose(extended[0], (1, 0, 2))
    value_heads = jnp.transpose(extended[1], (1, 0, 2))
    query_heads = jnp.transpose(query, (1, 0, 2))
    frame_block = lax.axis_index("tm")
    row_block = lax.axis_index("height")
    first_frame = frame_block * frame_count
    first_row = row_block * row_count
    zero = jnp.int32(0)
    valid_pad = jnp.pad(valid, ((TT, TT), (TH, TH), (0, 0)))
    key_valid = (
        lax.dynamic_slice(
            valid_pad, (first_frame, first_row, zero), (frames_ext, rows_ext, width)
        ).reshape(-1)
        > 0
    )
    query_valid = (
        lax.dynamic_slice(
            valid, (first_frame, first_row, zero), (frame_count, row_count, width)
        ).reshape(-1)
        > 0
    )
    query_coords = tile_coords(
        first_frame + jnp.arange(frame_count, dtype=jnp.int32),
        first_row + jnp.arange(row_count, dtype=jnp.int32),
        width,
    )
    key_coords = tile_coords(
        first_frame - TT + jnp.arange(frames_ext, dtype=jnp.int32),
        first_row - TH + jnp.arange(rows_ext, dtype=jnp.int32),
        width,
    )
    apart_t, apart_h, apart_w = (
        jnp.abs(qa[:, None] - ka[None, :]) for qa, ka in zip(query_coords, key_coords)
    )
    seen = key_valid[None, :]
    scale = 1.0 / jnp.sqrt(jnp.float32(HDIM))

    def per_head(inputs):
        query_one, key_one, value_one, reach = inputs
        allowed = (apart_t <= reach[0]) & (apart_h <= reach[1]) & (apart_w <= reach[2]) & seen
        scores = (
            jnp.einsum("qd,kd->qk", query_one, key_one, preferred_element_type=jnp.float32) * scale
        )
        terms = jnp.where(allowed, jnp.exp(scores), jnp.float32(0.0))
        total = jnp.sum(terms, axis=-1, keepdims=True)
        total = jnp.where(query_valid[:, None], total, jnp.float32(1.0))
        weights = (terms / total).astype(jnp.bfloat16)
        result = jnp.dot(weights, value_one, preferred_element_type=jnp.float32)
        return jnp.where(query_valid[:, None], result, jnp.float32(0.0)).astype(jnp.bfloat16)

    heads_out = lax.map(per_head, (query_heads, key_heads, value_heads, window))
    attended = jnp.transpose(heads_out, (1, 0, 2)).reshape(frame_count, row_count, width, inner)
    return attended


def solution(mesh):
    in_specs = (
        P("tm", "height", None, None),
        P(),
        P(),
        P(("tm", "height"), None),
        P(),
        P(),
        P(),
        P(),
    )
    out_specs = P("tm", "height", None, None)
    return jax.shard_map(
        per_device, mesh=mesh, in_specs=in_specs, out_specs=out_specs, check_vma=False
    )
```

profile of v0, /device:TPU:4, one launch (start us, length us, event | category | flops | bytes accessed | tf_op | source)
XLA Modules:
  0.0 750.8 jit_solution(9672114326475516388)
XLA Ops:
  18.4 334.2 %all-gather.2.cloned.1.call-done = bf16[3072,4608]{1,0:T(8,128)(2,1)} async-done(((bf16[24,4608]{1,0:T(8,128)(2,1)}), bf16[3072,4608]{1,0:T(8,128)(2,1)}) %all-gather.2.cloned.1.call-update) | async-done | bytes 28311568 | tf_op jit(solution)/shard_map/all_gather | solution.py:58
  352.6 23.6 %fusion.33 = f32[640,4608]{1,0:T(8,128)S(1)} fusion(bf16[640,3072]{1,0:T(8,128)(2,1)} %fusion.25, bf16[3072,4608]{1,0:T(8,128)(2,1)} %all-gather.2.cloned.1.call-done), kind=kOutput, calls=%fused_computation.72 | convolution fusion | flops 18119393280 | bytes 44040192 | tf_op jit(solution)/shard_map/dot_general | solution.py:59
  406.8 6.3 collective-permute-start.1
  413.1 20.4 %collective-permute-done = bf16[2,1,1,2,2,80,1536]{6,5,4,3,1,2,0:T(8,128)(2,1)S(1)} collective-permute-done((bf16[2,1,1,2,2,80,1536]{6,5,4,3,1,2,0:T(8,128)(2,1)S(1)}, bf16[2,1,1,2,2,80,1536]{6,5,4,3,1,2,0:T(8,128)(2,1)S(1)}, u32[]{:S(2)}, u32[]{:S(2)}) %collective-permute-start) | collective-permute-done | bytes 1966112 | tf_op jit(solution)/shard_map/ppermute | solution.py:22
  460.1 67.4 %collective-permute-done.2 = bf16[2,4,1,1,2,80,1536]{6,5,4,3,1,2,0:T(8,128)(2,1)} collective-permute-done((bf16[2,4,1,1,2,80,1536]{6,5,4,3,1,2,0:T(8,128)(2,1)}, bf16[2,4,1,1,2,80,1536]{6,5,4,3,1,2,0:T(8,128)(2,1)}, u32[]{:S(2)}, u32[]{:S(2)}) %collective-permute-start.2) | collective-permute-done | bytes 3932192 | tf_op jit(solution)/shard_map/ppermute | solution.py:22
  527.5 6.0 collective-permute-done.3
  533.4 6.5 pad_maximum_fusion
  545.7 15.1 %squeeze.28 = bf16[2560,12,128]{2,1,0:T(8,128)(2,1)} reshape(bf16[1,4,1,4,2,80,1536]{6,5,4,3,1,2,0:T(8,128)(2,1)} %get-tuple-element.149) | data formatting | bytes 15728640 | tf_op jit(solution)/shard_map/squeeze | solution.py:71
  560.8 9.2 %copy.16 = bf16[12,2560,128]{2,1,0:T(8,128)(2,1)} copy(bf16[12,2560,128]{2,0,1:T(8,128)(2,1)} %bitcast.66) | data formatting | bytes 15728640
  570.0 15.1 %squeeze.29 = bf16[2560,12,128]{2,1,0:T(8,128)(2,1)} reshape(bf16[1,4,1,4,2,80,1536]{6,5,4,3,1,2,0:T(8,128)(2,1)} %get-tuple-element.148) | data formatting | bytes 15728640 | tf_op jit(solution)/shard_map/squeeze | solution.py:72
  585.0 9.3 %copy.17 = bf16[12,2560,128]{2,1,0:T(8,128)(2,1)} copy(bf16[12,2560,128]{2,0,1:T(8,128)(2,1)} %bitcast.67) | data formatting | bytes 15728640
  594.3 142.9 %while.11 = (s32[]{:T(128)}, bf16[12,640,128]{2,1,0:T(8,128)(2,1)S(1)}, pred[640]{0:T(1024)(128)(4,1)S(1)}, s32[12,3]{0,1:T(4,128)S(1)}, pred[1,2560]{1,0:T(4,12...) while((s32[]{:T(128)}, ...), condition=%wide.region_6.7_spmd.clone, body=%wide.region_4.6_spmd.clone.sunk | while | flops 866877440 | bytes 14808906 | solution.py:121
  595.0 8.9 %fusion.42 = (f32[640]{0:T(1024)S(1)}, f32[640,2560]{1,0:T(8,128)S(1)}) fusion(bf16[12,2560,128]{2,1,0:T(8,128)(2,1)} %get-tuple-element.290, s32[]{:T(128)} %get-tuple-element.268, bf16[12,640,128]{1,2,0:T(8,128)(2,1)} %get-tuple-element.289, pred[2560]{0:T(1024)(128)(4,1)S(1)} %reduce.4, s32[]{:T(128)} %bitcast.63, ...), kind=kOutput, calls=%fused_computation.69.clone.1 | convolution fusion | flops 444005760 | bytes 7418880 | tf_op jit(solution)/shard_map/while/body/eval_jaxpr/qd,kd->qk/dot_general | solution.py:112
  606.9 8.9 %fusion.42 = (f32[640]{0:T(1024)S(1)}, f32[640,2560]{1,0:T(8,128)S(1)}) fusion(bf16[12,2560,128]{2,1,0:T(8,128)(2,1)} %get-tuple-element.290, s32[]{:T(128)} %get-tuple-element.268, bf16[12,640,128]{1,2,0:T(8,128)(2,1)} %get-tuple-element.289, pred[2560]{0:T(1024)(128)(4,1)S(1)} %reduce.4, s32[]{:T(128)} %bitcast.63, ...), kind=kOutput, calls=%fused_computation.69.clone.1 | convolution fusion | flops 444005760 | bytes 7418880 | tf_op jit(solution)/shard_map/while/body/eval_jaxpr/qd,kd->qk/dot_general | solution.py:112
  618.8 8.9 %fusion.42 = (f32[640]{0:T(1024)S(1)}, f32[640,2560]{1,0:T(8,128)S(1)}) fusion(bf16[12,2560,128]{2,1,0:T(8,128)(2,1)} %get-tuple-element.290, s32[]{:T(128)} %get-tuple-element.268, bf16[12,640,128]{1,2,0:T(8,128)(2,1)} %get-tuple-element.289, pred[2560]{0:T(1024)(128)(4,1)S(1)} %reduce.4, s32[]{:T(128)} %bitcast.63, ...), kind=kOutput, calls=%fused_computation.69.clone.1 | convolution fusion | flops 444005760 | bytes 7418880 | tf_op jit(solution)/shard_map/while/body/eval_jaxpr/qd,kd->qk/dot_general | solution.py:112
  630.7 8.9 %fusion.42 = (f32[640]{0:T(1024)S(1)}, f32[640,2560]{1,0:T(8,128)S(1)}) fusion(bf16[12,2560,128]{2,1,0:T(8,128)(2,1)} %get-tuple-element.290, s32[]{:T(128)} %get-tuple-element.268, bf16[12,640,128]{1,2,0:T(8,128)(2,1)} %get-tuple-element.289, pred[2560]{0:T(1024)(128)(4,1)S(1)} %reduce.4, s32[]{:T(128)} %bitcast.63, ...), kind=kOutput, calls=%fused_computation.69.clone.1 | convolution fusion | flops 444005760 | bytes 7418880 | tf_op jit(solution)/shard_map/while/body/eval_jaxpr/qd,kd->qk/dot_general | solution.py:112
  642.6 8.9 %fusion.42 = (f32[640]{0:T(1024)S(1)}, f32[640,2560]{1,0:T(8,128)S(1)}) fusion(bf16[12,2560,128]{2,1,0:T(8,128)(2,1)} %get-tuple-element.290, s32[]{:T(128)} %get-tuple-element.268, bf16[12,640,128]{1,2,0:T(8,128)(2,1)} %get-tuple-element.289, pred[2560]{0:T(1024)(128)(4,1)S(1)} %reduce.4, s32[]{:T(128)} %bitcast.63, ...), kind=kOutput, calls=%fused_computation.69.clone.1 | convolution fusion | flops 444005760 | bytes 7418880 | tf_op jit(solution)/shard_map/while/body/eval_jaxpr/qd,kd->qk/dot_general | solution.py:112
  654.5 8.9 %fusion.42 = (f32[640]{0:T(1024)S(1)}, f32[640,2560]{1,0:T(8,128)S(1)}) fusion(bf16[12,2560,128]{2,1,0:T(8,128)(2,1)} %get-tuple-element.290, s32[]{:T(128)} %get-tuple-element.268, bf16[12,640,128]{1,2,0:T(8,128)(2,1)} %get-tuple-element.289, pred[2560]{0:T(1024)(128)(4,1)S(1)} %reduce.4, s32[]{:T(128)} %bitcast.63, ...), kind=kOutput, calls=%fused_computation.69.clone.1 | convolution fusion | flops 444005760 | bytes 7418880 | tf_op jit(solution)/shard_map/while/body/eval_jaxpr/qd,kd->qk/dot_general | solution.py:112
  666.5 8.9 %fusion.42 = (f32[640]{0:T(1024)S(1)}, f32[640,2560]{1,0:T(8,128)S(1)}) fusion(bf16[12,2560,128]{2,1,0:T(8,128)(2,1)} %get-tuple-element.290, s32[]{:T(128)} %get-tuple-element.268, bf16[12,640,128]{1,2,0:T(8,128)(2,1)} %get-tuple-element.289, pred[2560]{0:T(1024)(128)(4,1)S(1)} %reduce.4, s32[]{:T(128)} %bitcast.63, ...), kind=kOutput, calls=%fused_computation.69.clone.1 | convolution fusion | flops 444005760 | bytes 7418880 | tf_op jit(solution)/shard_map/while/body/eval_jaxpr/qd,kd->qk/dot_general | solution.py:112
  678.4 8.9 %fusion.42 = (f32[640]{0:T(1024)S(1)}, f32[640,2560]{1,0:T(8,128)S(1)}) fusion(bf16[12,2560,128]{2,1,0:T(8,128)(2,1)} %get-tuple-element.290, s32[]{:T(128)} %get-tuple-element.268, bf16[12,640,128]{1,2,0:T(8,128)(2,1)} %get-tuple-element.289, pred[2560]{0:T(1024)(128)(4,1)S(1)} %reduce.4, s32[]{:T(128)} %bitcast.63, ...), kind=kOutput, calls=%fused_computation.69.clone.1 | convolution fusion | flops 444005760 | bytes 7418880 | tf_op jit(solution)/shard_map/while/body/eval_jaxpr/qd,kd->qk/dot_general | solution.py:112
  690.3 8.9 %fusion.42 = (f32[640]{0:T(1024)S(1)}, f32[640,2560]{1,0:T(8,128)S(1)}) fusion(bf16[12,2560,128]{2,1,0:T(8,128)(2,1)} %get-tuple-element.290, s32[]{:T(128)} %get-tuple-element.268, bf16[12,640,128]{1,2,0:T(8,128)(2,1)} %get-tuple-element.289, pred[2560]{0:T(1024)(128)(4,1)S(1)} %reduce.4, s32[]{:T(128)} %bitcast.63, ...), kind=kOutput, calls=%fused_computation.69.clone.1 | convolution fusion | flops 444005760 | bytes 7418880 | tf_op jit(solution)/shard_map/while/body/eval_jaxpr/qd,kd->qk/dot_general | solution.py:112
  702.2 8.9 %fusion.42 = (f32[640]{0:T(1024)S(1)}, f32[640,2560]{1,0:T(8,128)S(1)}) fusion(bf16[12,2560,128]{2,1,0:T(8,128)(2,1)} %get-tuple-element.290, s32[]{:T(128)} %get-tuple-element.268, bf16[12,640,128]{1,2,0:T(8,128)(2,1)} %get-tuple-element.289, pred[2560]{0:T(1024)(128)(4,1)S(1)} %reduce.4, s32[]{:T(128)} %bitcast.63, ...), kind=kOutput, calls=%fused_computation.69.clone.1 | convolution fusion | flops 444005760 | bytes 7418880 | tf_op jit(solution)/shard_map/while/body/eval_jaxpr/qd,kd->qk/dot_general | solution.py:112
  714.1 8.9 %fusion.42 = (f32[640]{0:T(1024)S(1)}, f32[640,2560]{1,0:T(8,128)S(1)}) fusion(bf16[12,2560,128]{2,1,0:T(8,128)(2,1)} %get-tuple-element.290, s32[]{:T(128)} %get-tuple-element.268, bf16[12,640,128]{1,2,0:T(8,128)(2,1)} %get-tuple-element.289, pred[2560]{0:T(1024)(128)(4,1)S(1)} %reduce.4, s32[]{:T(128)} %bitcast.63, ...), kind=kOutput, calls=%fused_computation.69.clone.1 | convolution fusion | flops 444005760 | bytes 7418880 | tf_op jit(solution)/shard_map/while/body/eval_jaxpr/qd,kd->qk/dot_general | solution.py:112
  726.0 8.9 %fusion.42 = (f32[640]{0:T(1024)S(1)}, f32[640,2560]{1,0:T(8,128)S(1)}) fusion(bf16[12,2560,128]{2,1,0:T(8,128)(2,1)} %get-tuple-element.290, s32[]{:T(128)} %get-tuple-element.268, bf16[12,640,128]{1,2,0:T(8,128)(2,1)} %get-tuple-element.289, pred[2560]{0:T(1024)(128)(4,1)S(1)} %reduce.4, s32[]{:T(128)} %bitcast.63, ...), kind=kOutput, calls=%fused_computation.69.clone.1 | convolution fusion | flops 444005760 | bytes 7418880 | tf_op jit(solution)/shard_map/while/body/eval_jaxpr/qd,kd->qk/dot_general | solution.py:112
  (148 shorter events, 116.7 us)
Async XLA Ops:
  6.5 7.0 copy-start
  6.5 346.1 %all-gather.2.cloned.1.call-start = ((), (), s32[]{:S(2)}) async-start(), calls=%async_computation | async-start | bytes 28532736 | tf_op jit(solution)/shard_map/all_gather | solution.py:58
  7.3 6.3 copy-start.13
  7.3 6.3 copy-start.14
  403.5 31.7 %copy-start.3 = (bf16[1,2,1,2,2,80,1536]{6,5,4,3,1,2,0:T(8,128)(2,1)}, bf16[1,2,1,2,2,80,1536]{6,5,4,3,1,2,0:T(8,128)(2,1)S(1)}, u32[]{:S(2)}) copy-start(bf16[1,2,1,2,2,80,1536]{6,5,4,3,1,2,0:T(8,128)(2,1)S(1)} %multiply_convert_fusion) | copy-start | bytes 5898244
  403.9 29.6 %collective-permute-start = (bf16[2,1,1,2,2,80,1536]{6,5,4,3,1,2,0:T(8,128)(2,1)S(1)}, bf16[2,1,1,2,2,80,1536]{6,5,4,3,1,2,0:T(8,128)(2,1)S(1)}, u32[]{:S(2)}, u32[]{:S(2)}) collective-permute-start(bf16[2,1,1,2,2,80,1536]{6,5,4,3,1,2,0:T(8,128)(2,1)S(1)} %get-tuple-element.155), channel_id=1, source_target_pairs={{0,8},{8,16},{16,24},{24,32},{32,40},{40,48},{48,56},{56,64},{64,7... | collective-permute-start | bytes 5898248 | tf_op jit(solution)/shard_map/ppermute | solution.py:22
  406.8 28.5 %collective-permute-start.1 = (bf16[2,1,1,2,2,80,1536]{6,5,4,3,1,2,0:T(8,128)(2,1)S(1)}, bf16[2,1,1,2,2,80,1536]{6,5,4,3,1,2,0:T(8,128)(2,1)S(1)}, u32[]{:S(2)}, u32[]{:S(2)}) collective-permute-start(bf16[2,1,1,2,2,80,1536]{6,5,4,3,1,2,0:T(8,128)(2,1)S(1)} %get-tuple-element.156), channel_id=1, source_target_pairs={{8,0},{16,8},{24,16},{32,24},{40,32},{48,40},{56,48},{64,56},{72,6... | collective-permute-start | bytes 5898248 | tf_op jit(solution)/shard_map/ppermute | solution.py:24
  433.5 1.8 copy-start.5
  435.3 1.3 copy-start.7
  437.6 10.7 %copy-start.11 = (s32[32,32,80]{2,1,0:T(8,128)S(1)}, s32[32,32,80]{2,1,0:T(8,128)}, u32[]{:S(2)}) copy-start(s32[32,32,80]{2,1,0:T(8,128)} %param.17) | copy-start | bytes 983044
  441.1 86.4 %collective-permute-start.2 = (bf16[2,4,1,1,2,80,1536]{6,5,4,3,1,2,0:T(8,128)(2,1)}, bf16[2,4,1,1,2,80,1536]{6,5,4,3,1,2,0:T(8,128)(2,1)}, u32[]{:S(2)}, u32[]{:S(2)}) collective-permute-start(bf16[2,4,1,1,2,80,1536]{6,5,4,3,1,2,0:T(8,128)(2,1)} %get-tuple-element.153), channel_id=1, source_target_pairs={{0,1},{1,2},{2,3},{3,4},{4,5},{5,6},{6,7},{8,9},{9,10},{10,11},{11... | collective-permute-start | bytes 11796488 | tf_op jit(solution)/shard_map/ppermute | solution.py:22
  446.8 86.6 %collective-permute-start.3 = (bf16[2,4,1,1,2,80,1536]{6,5,4,3,1,2,0:T(8,128)(2,1)}, bf16[2,4,1,1,2,80,1536]{6,5,4,3,1,2,0:T(8,128)(2,1)}, u32[]{:S(2)}, u32[]{:S(2)}) collective-permute-start(bf16[2,4,1,1,2,80,1536]{6,5,4,3,1,2,0:T(8,128)(2,1)} %get-tuple-element.154), channel_id=1, source_target_pairs={{1,0},{2,1},{3,2},{4,3},{5,4},{6,5},{7,6},{9,8},{10,9},{11,10},{12... | collective-permute-start | bytes 11796488 | tf_op jit(solution)/shard_map/ppermute | solution.py:24
  454.9 3.3 copy-start.2
  454.9 3.3 copy-start.15
  457.5 76.0 %copy-start.4 = (bf16[1,2,1,2,2,80,1536]{6,5,4,3,1,2,0:T(8,128)(2,1)S(1)}, bf16[1,2,1,2,2,80,1536]{6,5,4,3,1,2,0:T(8,128)(2,1)}, u32[]{:S(2)}) copy-start(bf16[1,2,1,2,2,80,1536]{6,5,4,3,1,2,0:T(8,128)(2,1)} %copy-done.3) | copy-start | bytes 5898244
  457.5 76.0 %copy-start.6 = (bf16[2,1,1,2,2,80,1536]{6,5,4,3,1,2,0:T(8,128)(2,1)S(1)}, bf16[2,1,1,2,2,80,1536]{6,5,4,3,1,2,0:T(8,128)(2,1)}, u32[]{:S(2)}) copy-start(bf16[2,1,1,2,2,80,1536]{6,5,4,3,1,2,0:T(8,128)(2,1)} %copy-done.5) | copy-start | bytes 5898244
  457.5 76.0 %copy-start.8 = (bf16[2,1,1,2,2,80,1536]{6,5,4,3,1,2,0:T(8,128)(2,1)S(1)}, bf16[2,1,1,2,2,80,1536]{6,5,4,3,1,2,0:T(8,128)(2,1)}, u32[]{:S(2)}) copy-start(bf16[2,1,1,2,2,80,1536]{6,5,4,3,1,2,0:T(8,128)(2,1)} %copy-done.7) | copy-start | bytes 5898244
  585.0 9.3 %copy-start.9 = (bf16[12,640,128]{2,1,0:T(8,128)(2,1)S(1)}, bf16[12,640,128]{2,1,0:T(8,128)(2,1)}, u32[]{:S(2)}) copy-start(bf16[12,640,128]{2,1,0:T(8,128)(2,1)} %custom-call) | copy-start | bytes 5898244
  585.0 9.3 %copy-start.12 = (s32[12,3]{0,1:T(4,128)S(1)}, s32[12,3]{0,1:T(4,128)}, u32[]{:S(2)}) copy-start(s32[12,3]{0,1:T(4,128)} %param.16) | copy-start | bytes 436
  737.2 1.3 copy-start.10
  738.5 5.5 copy-start.1
Sparse Core Ops, SparseCore 0:
  9.1 343.5 all-gather.1
where the time goes:
time: 753 us; the launch traced here: 751 us
  waiting for transfers between devices  430 us (57%)
  matrix products  158 us (21%)
  local copies, waits for them, and re-layouts  96.6 us (13%)
  other arithmetic  35.8 us (5%)
  starting transfers between devices  16.4 us (2%)
  between operations  13.7 us (2%)
    all_gather x1, waiting for transfers between devices, per_device(): full_weight = lax.all_gather(w_qkv, ('tm', 'height'), axis=0, tiled=True)  334 us
    dot_general x12, matrix products, per_head(): jnp.einsum('qd,kd->qk', query_one, key_one, preferred_element_type=jnp.fl...  107 us
    ppermute x2, waiting for transfers between devices, with_halo(): lax.ppermute(tail, axis, [(i, (i + 1) % count) for i in range(ends)])  87.7 us
    dot_general x12, matrix products, per_head(): result = jnp.dot(weights, value_one, preferred_element_type=jnp.float32)  26.8 us
    dot_general x1, matrix products, per_device(): qkv = jnp.dot(modulated, full_weight, preferred_element_type=jnp.float32)  23.6 us
    unnamed x34, local copies, waits for them, and re-layouts  21.7 us
    squeeze x1, local copies, waits for them, and re-layouts, per_device(): key_heads = jnp.transpose(extended[0], (1, 0, 2))  15.1 us
    squeeze x1, local copies, waits for them, and re-layouts, per_device(): value_heads = jnp.transpose(extended[1], (1, 0, 2))  15.1 us
  transfers between devices with their start and end apart: 5, of which 5 were waited for; matrix products, arithmetic and copies ran while one was open for 3% of the time, Pallas kernels for 0%

commit v1 on v0

--- a/solution.py
+++ b/solution.py
@@ -55,7 +55,12 @@
     frame_count, row_count, width, features = tokens.shape
     token_count = frame_count * row_count * width
     modulated = modulate(tokens.reshape(token_count, features), mod_scale, mod_shift)
-    full_weight = lax.all_gather(w_qkv, ("tm", "height"), axis=0, tiled=True)
+    full_weight = jnp.concatenate(
+        lax.all_to_all(
+            jnp.stack([w_qkv] * lax.axis_size(("tm", "height"))), ("tm", "height"), 0, 0
+        ),
+        axis=0,
+    )
     qkv = jnp.dot(modulated, full_weight, preferred_element_type=jnp.float32)
     inner = qkv.shape[1] // 3
     query = head_norm(qkv[:, :inner].reshape(token_count, HEADS, HDIM), q_gain)

time: 753 us -> 847 us (1.12)
  waiting for transfers between devices: 430 us -> 495 us
  starting transfers between devices: 16.4 us -> 47.2 us
  between operations: 13.7 us -> 0.34 us
  local copies, waits for them, and re-layouts: 96.6 us -> 107 us
    all_to_all x0 -> x1, waiting for transfers between devices: none -> 415 us  [per_device(): lax.all_to_all(jnp.stack([w_qkv] * lax.axis_size(('tm', 'height'))), ('tm...]
    all_gather x1 -> x0, waiting for transfers between devices: 334 us -> none  [per_device(): full_weight = lax.all_gather(w_qkv, ('tm', 'height'), axis=0, tiled=True)]
    ppermute x2, starting transfers between devices: 8.63 us -> 26.6 us  [with_halo(): lax.ppermute(tail, axis, [(i, (i + 1) % count) for i in range(ends)])]
    ppermute x2, waiting for transfers between devices: 87.7 us -> 71.4 us  [with_halo(): lax.ppermute(tail, axis, [(i, (i + 1) % count) for i in range(ends)])]
    all_to_all x0 -> x1, starting transfers between devices: none -> 10.9 us  [per_device(): lax.all_to_all(jnp.stack([w_qkv] * lax.axis_size(('tm', 'height'))), ('tm...]
    another operation x0 -> x1, local copies, waits for them, and re-layouts: none -> 10.3 us  [per_device(): jnp.stack([w_qkv] * lax.axis_size(('tm', 'height')))]
    unnamed x34 -> x36, local copies, waits for them, and re-layouts: 21.7 us -> 22.2 us
  transfers between devices with their start and end apart: 5 -> 5, of which waited for: 5 -> 5; matrix products, arithmetic and copies ran while one was open for 3% -> 2% of each run, Pallas kernels for 0% -> 0%
where the time goes in v1:
time: 847 us; the launch traced here: 839 us
  waiting for transfers between devices  495 us (58%)
  matrix products  157 us (19%)
  local copies, waits for them, and re-layouts  107 us (13%)
  starting transfers between devices  47.2 us (6%)
  other arithmetic  32.4 us (4%)
    all_to_all x1, waiting for transfers between devices, per_device(): lax.all_to_all(jnp.stack([w_qkv] * lax.axis_size(('tm', 'height'))), ('tm...  415 us
    dot_general x12, matrix products, per_head(): jnp.einsum('qd,kd->qk', query_one, key_one, preferred_element_type=jnp.fl...  107 us
    ppermute x2, waiting for transfers between devices, with_halo(): lax.ppermute(tail, axis, [(i, (i + 1) % count) for i in range(ends)])  71.4 us
    dot_general x12, matrix products, per_head(): result = jnp.dot(weights, value_one, preferred_element_type=jnp.float32)  26.7 us
    ppermute x2, starting transfers between devices, with_halo(): lax.ppermute(tail, axis, [(i, (i + 1) % count) for i in range(ends)])  26.6 us
    dot_general x1, matrix products, per_device(): qkv = jnp.dot(modulated, full_weight, preferred_element_type=jnp.float32)  23.6 us
    unnamed x36, local copies, waits for them, and re-layouts  22.2 us
  transfers between devices with their start and end apart: 5, of which 5 were waited for; matrix products, arithmetic and copies ran while one was open for 2% of the time, Pallas kernels for 0%

profile of v1, /device:TPU:4, one launch (start us, length us, event | category | flops | bytes accessed | tf_op | source)
XLA Modules:
  0.0 839.2 jit_solution(18426470937499192064)
XLA Ops:
  0.0 10.3 %stack.4 = bf16[128,24,4608]{2,1,0:T(8,128)(2,1)} broadcast(bf16[24,4608]{1,0:T(8,128)(2,1)} %param.13), dimensions={1,2} | broadcast | bytes 28532736 | tf_op jit(solution)/shard_map/stack | solution.py:60
  10.3 10.9 %all-to-all-start = ((bf16[128,24,4608]{2,1,0:T(8,128)(2,1)}), bf16[128,24,4608]{2,1,0:T(8,128)(2,1)}, u32[]{:S(2)}, u32[]{:S(2)}) async-start(bf16[128,24,4608]{2,1,0:T(8,128)(2,1)} %stack.4), calls=%async_computation | async-start | bytes 56623104 | tf_op jit(solution)/shard_map/all_to_all | solution.py:59
  29.1 415.0 %all-to-all-done = bf16[128,24,4608]{2,1,0:T(8,128)(2,1)} async-done(((bf16[128,24,4608]{2,1,0:T(8,128)(2,1)}), bf16[128,24,4608]{2,1,0:T(8,128)(2,1)}, u32[]{:S(2)}, u32[]{:S(2)}) %all-to-all-start) | async-done | bytes 28311584 | tf_op jit(solution)/shard_map/all_to_all | solution.py:59
  444.1 23.6 %fusion.35 = f32[640,4608]{1,0:T(8,128)S(1)} fusion(bf16[640,3072]{1,0:T(8,128)(2,1)} %bitcast.67, bf16[3072,4608]{1,0:T(8,128)(2,1)} %bitcast.1), kind=kOutput, calls=%fused_computation.73 | convolution fusion | flops 18119393280 | bytes 44040192 | tf_op jit(solution)/shard_map/dot_general | solution.py:64
  511.3 20.2 %collective-permute-done = bf16[2,1,1,2,2,80,1536]{6,5,4,3,1,2,0:T(8,128)(2,1)S(1)} collective-permute-done((bf16[2,1,1,2,2,80,1536]{6,5,4,3,1,2,0:T(8,128)(2,1)S(1)}, bf16[2,1,1,2,2,80,1536]{6,5,4,3,1,2,0:T(8,128)(2,1)S(1)}, u32[]{:S(2)}, u32[]{:S(2)}) %collective-permute-start) | collective-permute-done | bytes 1966112 | tf_op jit(solution)/shard_map/ppermute | solution.py:22
  539.1 19.1 %collective-permute-start.2 = (bf16[2,4,1,1,2,80,1536]{6,5,4,3,1,2,0:T(8,128)(2,1)}, bf16[2,4,1,1,2,80,1536]{6,5,4,3,1,2,0:T(8,128)(2,1)}, u32[]{:S(2)}, u32[]{:S(2)}) collective-permute-start(bf16[2,4,1,1,2,80,1536]{6,5,4,3,1,2,0:T(8,128)(2,1)} %get-tuple-element.153), channel_id=1, source_target_pairs={{0,1},{1,2},{2,3},{3,4},{4,5},{5,6},{6,7},{8,9},{9,10},{10,11},{11... | collective-permute-start | bytes 11796488 | tf_op jit(solution)/shard_map/ppermute | solution.py:22
  571.2 51.2 %collective-permute-done.2 = bf16[2,4,1,1,2,80,1536]{6,5,4,3,1,2,0:T(8,128)(2,1)} collective-permute-done((bf16[2,4,1,1,2,80,1536]{6,5,4,3,1,2,0:T(8,128)(2,1)}, bf16[2,4,1,1,2,80,1536]{6,5,4,3,1,2,0:T(8,128)(2,1)}, u32[]{:S(2)}, u32[]{:S(2)}) %collective-permute-start.2) | collective-permute-done | bytes 3932192 | tf_op jit(solution)/shard_map/ppermute | solution.py:22
  641.4 15.1 %squeeze.28 = bf16[2560,12,128]{2,1,0:T(8,128)(2,1)} reshape(bf16[1,4,1,4,2,80,1536]{6,5,4,3,1,2,0:T(8,128)(2,1)} %get-tuple-element.149) | data formatting | bytes 15728640 | tf_op jit(solution)/shard_map/squeeze | solution.py:76
  656.5 9.1 %copy.16 = bf16[12,2560,128]{2,1,0:T(8,128)(2,1)} copy(bf16[12,2560,128]{2,0,1:T(8,128)(2,1)} %bitcast.58) | data formatting | bytes 15728640
  665.7 15.1 %squeeze.29 = bf16[2560,12,128]{2,1,0:T(8,128)(2,1)} reshape(bf16[1,4,1,4,2,80,1536]{6,5,4,3,1,2,0:T(8,128)(2,1)} %get-tuple-element.148) | data formatting | bytes 15728640 | tf_op jit(solution)/shard_map/squeeze | solution.py:77
  680.8 9.3 %copy.17 = bf16[12,2560,128]{2,1,0:T(8,128)(2,1)} copy(bf16[12,2560,128]{2,0,1:T(8,128)(2,1)} %bitcast.59) | data formatting | bytes 15728640
  690.1 142.3 %while.11 = (s32[]{:T(128)}, bf16[12,640,128]{2,1,0:T(8,128)(2,1)S(1)}, pred[640]{0:T(1024)(128)(4,1)S(1)}, s32[12,3]{0,1:T(4,128)S(1)}, pred[1,2560]{1,0:T(4,12...) while((s32[]{:T(128)}, ...), condition=%wide.region_6.7_spmd.clone, body=%wide.region_4.6_spmd.clone.sunk | while | flops 866877440 | bytes 14808906 | solution.py:126
  690.8 8.9 %fusion.44 = (f32[640]{0:T(1024)S(1)}, f32[640,2560]{1,0:T(8,128)S(1)}) fusion(bf16[12,2560,128]{2,1,0:T(8,128)(2,1)} %get-tuple-element.290, s32[]{:T(128)} %get-tuple-element.268, bf16[12,640,128]{1,2,0:T(8,128)(2,1)} %get-tuple-element.289, pred[2560]{0:T(1024)(128)(4,1)S(1)} %reduce.4, s32[]{:T(128)} %bitcast.55, ...), kind=kOutput, calls=%fused_computation.70.clone.1 | convolution fusion | flops 444005760 | bytes 7418880 | tf_op jit(solution)/shard_map/while/body/eval_jaxpr/qd,kd->qk/dot_general | solution.py:117
  702.6 8.9 %fusion.44 = (f32[640]{0:T(1024)S(1)}, f32[640,2560]{1,0:T(8,128)S(1)}) fusion(bf16[12,2560,128]{2,1,0:T(8,128)(2,1)} %get-tuple-element.290, s32[]{:T(128)} %get-tuple-element.268, bf16[12,640,128]{1,2,0:T(8,128)(2,1)} %get-tuple-element.289, pred[2560]{0:T(1024)(128)(4,1)S(1)} %reduce.4, s32[]{:T(128)} %bitcast.55, ...), kind=kOutput, calls=%fused_computation.70.clone.1 | convolution fusion | flops 444005760 | bytes 7418880 | tf_op jit(solution)/shard_map/while/body/eval_jaxpr/qd,kd->qk/dot_general | solution.py:117
  714.5 8.9 %fusion.44 = (f32[640]{0:T(1024)S(1)}, f32[640,2560]{1,0:T(8,128)S(1)}) fusion(bf16[12,2560,128]{2,1,0:T(8,128)(2,1)} %get-tuple-element.290, s32[]{:T(128)} %get-tuple-element.268, bf16[12,640,128]{1,2,0:T(8,128)(2,1)} %get-tuple-element.289, pred[2560]{0:T(1024)(128)(4,1)S(1)} %reduce.4, s32[]{:T(128)} %bitcast.55, ...), kind=kOutput, calls=%fused_computation.70.clone.1 | convolution fusion | flops 444005760 | bytes 7418880 | tf_op jit(solution)/shard_map/while/body/eval_jaxpr/qd,kd->qk/dot_general | solution.py:117
  726.3 8.9 %fusion.44 = (f32[640]{0:T(1024)S(1)}, f32[640,2560]{1,0:T(8,128)S(1)}) fusion(bf16[12,2560,128]{2,1,0:T(8,128)(2,1)} %get-tuple-element.290, s32[]{:T(128)} %get-tuple-element.268, bf16[12,640,128]{1,2,0:T(8,128)(2,1)} %get-tuple-element.289, pred[2560]{0:T(1024)(128)(4,1)S(1)} %reduce.4, s32[]{:T(128)} %bitcast.55, ...), kind=kOutput, calls=%fused_computation.70.clone.1 | convolution fusion | flops 444005760 | bytes 7418880 | tf_op jit(solution)/shard_map/while/body/eval_jaxpr/qd,kd->qk/dot_general | solution.py:117
  738.2 8.9 %fusion.44 = (f32[640]{0:T(1024)S(1)}, f32[640,2560]{1,0:T(8,128)S(1)}) fusion(bf16[12,2560,128]{2,1,0:T(8,128)(2,1)} %get-tuple-element.290, s32[]{:T(128)} %get-tuple-element.268, bf16[12,640,128]{1,2,0:T(8,128)(2,1)} %get-tuple-element.289, pred[2560]{0:T(1024)(128)(4,1)S(1)} %reduce.4, s32[]{:T(128)} %bitcast.55, ...), kind=kOutput, calls=%fused_computation.70.clone.1 | convolution fusion | flops 444005760 | bytes 7418880 | tf_op jit(solution)/shard_map/while/body/eval_jaxpr/qd,kd->qk/dot_general | solution.py:117
  750.1 8.9 %fusion.44 = (f32[640]{0:T(1024)S(1)}, f32[640,2560]{1,0:T(8,128)S(1)}) fusion(bf16[12,2560,128]{2,1,0:T(8,128)(2,1)} %get-tuple-element.290, s32[]{:T(128)} %get-tuple-element.268, bf16[12,640,128]{1,2,0:T(8,128)(2,1)} %get-tuple-element.289, pred[2560]{0:T(1024)(128)(4,1)S(1)} %reduce.4, s32[]{:T(128)} %bitcast.55, ...), kind=kOutput, calls=%fused_computation.70.clone.1 | convolution fusion | flops 444005760 | bytes 7418880 | tf_op jit(solution)/shard_map/while/body/eval_jaxpr/qd,kd->qk/dot_general | solution.py:117
  761.9 8.9 %fusion.44 = (f32[640]{0:T(1024)S(1)}, f32[640,2560]{1,0:T(8,128)S(1)}) fusion(bf16[12,2560,128]{2,1,0:T(8,128)(2,1)} %get-tuple-element.290, s32[]{:T(128)} %get-tuple-element.268, bf16[12,640,128]{1,2,0:T(8,128)(2,1)} %get-tuple-element.289, pred[2560]{0:T(1024)(128)(4,1)S(1)} %reduce.4, s32[]{:T(128)} %bitcast.55, ...), kind=kOutput, calls=%fused_computation.70.clone.1 | convolution fusion | flops 444005760 | bytes 7418880 | tf_op jit(solution)/shard_map/while/body/eval_jaxpr/qd,kd->qk/dot_general | solution.py:117
  773.8 8.9 %fusion.44 = (f32[640]{0:T(1024)S(1)}, f32[640,2560]{1,0:T(8,128)S(1)}) fusion(bf16[12,2560,128]{2,1,0:T(8,128)(2,1)} %get-tuple-element.290, s32[]{:T(128)} %get-tuple-element.268, bf16[12,640,128]{1,2,0:T(8,128)(2,1)} %get-tuple-element.289, pred[2560]{0:T(1024)(128)(4,1)S(1)} %reduce.4, s32[]{:T(128)} %bitcast.55, ...), kind=kOutput, calls=%fused_computation.70.clone.1 | convolution fusion | flops 444005760 | bytes 7418880 | tf_op jit(solution)/shard_map/while/body/eval_jaxpr/qd,kd->qk/dot_general | solution.py:117
  785.6 8.9 %fusion.44 = (f32[640]{0:T(1024)S(1)}, f32[640,2560]{1,0:T(8,128)S(1)}) fusion(bf16[12,2560,128]{2,1,0:T(8,128)(2,1)} %get-tuple-element.290, s32[]{:T(128)} %get-tuple-element.268, bf16[12,640,128]{1,2,0:T(8,128)(2,1)} %get-tuple-element.289, pred[2560]{0:T(1024)(128)(4,1)S(1)} %reduce.4, s32[]{:T(128)} %bitcast.55, ...), kind=kOutput, calls=%fused_computation.70.clone.1 | convolution fusion | flops 444005760 | bytes 7418880 | tf_op jit(solution)/shard_map/while/body/eval_jaxpr/qd,kd->qk/dot_general | solution.py:117
  797.5 8.9 %fusion.44 = (f32[640]{0:T(1024)S(1)}, f32[640,2560]{1,0:T(8,128)S(1)}) fusion(bf16[12,2560,128]{2,1,0:T(8,128)(2,1)} %get-tuple-element.290, s32[]{:T(128)} %get-tuple-element.268, bf16[12,640,128]{1,2,0:T(8,128)(2,1)} %get-tuple-element.289, pred[2560]{0:T(1024)(128)(4,1)S(1)} %reduce.4, s32[]{:T(128)} %bitcast.55, ...), kind=kOutput, calls=%fused_computation.70.clone.1 | convolution fusion | flops 444005760 | bytes 7418880 | tf_op jit(solution)/shard_map/while/body/eval_jaxpr/qd,kd->qk/dot_general | solution.py:117
  809.3 8.9 %fusion.44 = (f32[640]{0:T(1024)S(1)}, f32[640,2560]{1,0:T(8,128)S(1)}) fusion(bf16[12,2560,128]{2,1,0:T(8,128)(2,1)} %get-tuple-element.290, s32[]{:T(128)} %get-tuple-element.268, bf16[12,640,128]{1,2,0:T(8,128)(2,1)} %get-tuple-element.289, pred[2560]{0:T(1024)(128)(4,1)S(1)} %reduce.4, s32[]{:T(128)} %bitcast.55, ...), kind=kOutput, calls=%fused_computation.70.clone.1 | convolution fusion | flops 444005760 | bytes 7418880 | tf_op jit(solution)/shard_map/while/body/eval_jaxpr/qd,kd->qk/dot_general | solution.py:117
  821.2 8.9 %fusion.44 = (f32[640]{0:T(1024)S(1)}, f32[640,2560]{1,0:T(8,128)S(1)}) fusion(bf16[12,2560,128]{2,1,0:T(8,128)(2,1)} %get-tuple-element.290, s32[]{:T(128)} %get-tuple-element.268, bf16[12,640,128]{1,2,0:T(8,128)(2,1)} %get-tuple-element.289, pred[2560]{0:T(1024)(128)(4,1)S(1)} %reduce.4, s32[]{:T(128)} %bitcast.55, ...), kind=kOutput, calls=%fused_computation.70.clone.1 | convolution fusion | flops 444005760 | bytes 7418880 | tf_op jit(solution)/shard_map/while/body/eval_jaxpr/qd,kd->qk/dot_general | solution.py:117
  (148 shorter events, 132.4 us)
Async XLA Ops:
  0.0 25.7 %copy-start = (f32[128]{0:T(128)S(1)}, f32[128]{0:T(128)}, u32[]{:S(2)}) copy-start(f32[128]{0:T(128)} %param.15) | copy-start | bytes 1540
  10.3 433.8 %all-to-all-start = ((bf16[128,24,4608]{2,1,0:T(8,128)(2,1)}), bf16[128,24,4608]{2,1,0:T(8,128)(2,1)}, u32[]{:S(2)}, u32[]{:S(2)}) async-start(bf16[128,24,4608]{2,1,0:T(8,128)(2,1)} %stack.4), calls=%async_computation | async-start | bytes 56623104 | tf_op jit(solution)/shard_map/all_to_all | solution.py:59
  21.2 3.3 copy-start.2
  21.2 4.5 copy-start.14
  21.2 4.5 copy-start.15
  495.0 38.2 %copy-start.4 = (bf16[1,2,1,2,2,80,1536]{6,5,4,3,1,2,0:T(8,128)(2,1)}, bf16[1,2,1,2,2,80,1536]{6,5,4,3,1,2,0:T(8,128)(2,1)S(1)}, u32[]{:S(2)}) copy-start(bf16[1,2,1,2,2,80,1536]{6,5,4,3,1,2,0:T(8,128)(2,1)S(1)} %multiply_convert_fusion) | copy-start | bytes 5898244
  495.4 36.1 %collective-permute-start = (bf16[2,1,1,2,2,80,1536]{6,5,4,3,1,2,0:T(8,128)(2,1)S(1)}, bf16[2,1,1,2,2,80,1536]{6,5,4,3,1,2,0:T(8,128)(2,1)S(1)}, u32[]{:S(2)}, u32[]{:S(2)}) collective-permute-start(bf16[2,1,1,2,2,80,1536]{6,5,4,3,1,2,0:T(8,128)(2,1)S(1)} %get-tuple-element.155), channel_id=1, source_target_pairs={{0,8},{8,16},{16,24},{24,32},{32,40},{40,48},{48,56},{56,64},{64,7... | collective-permute-start | bytes 5898248 | tf_op jit(solution)/shard_map/ppermute | solution.py:22
  502.9 30.4 %collective-permute-start.1 = (bf16[2,1,1,2,2,80,1536]{6,5,4,3,1,2,0:T(8,128)(2,1)S(1)}, bf16[2,1,1,2,2,80,1536]{6,5,4,3,1,2,0:T(8,128)(2,1)S(1)}, u32[]{:S(2)}, u32[]{:S(2)}) collective-permute-start(bf16[2,1,1,2,2,80,1536]{6,5,4,3,1,2,0:T(8,128)(2,1)S(1)} %get-tuple-element.156), channel_id=1, source_target_pairs={{8,0},{16,8},{24,16},{32,24},{40,32},{48,40},{56,48},{64,56},{72,6... | collective-permute-start | bytes 5898248 | tf_op jit(solution)/shard_map/ppermute | solution.py:24
  531.5 1.8 copy-start.6
  533.2 1.4 copy-start.8
  535.7 23.8 %copy-start.12 = (s32[32,32,80]{2,1,0:T(8,128)S(1)}, s32[32,32,80]{2,1,0:T(8,128)}, u32[]{:S(2)}) copy-start(s32[32,32,80]{2,1,0:T(8,128)} %param.17) | copy-start | bytes 983044
  539.1 83.4 %collective-permute-start.2 = (bf16[2,4,1,1,2,80,1536]{6,5,4,3,1,2,0:T(8,128)(2,1)}, bf16[2,4,1,1,2,80,1536]{6,5,4,3,1,2,0:T(8,128)(2,1)}, u32[]{:S(2)}, u32[]{:S(2)}) collective-permute-start(bf16[2,4,1,1,2,80,1536]{6,5,4,3,1,2,0:T(8,128)(2,1)} %get-tuple-element.153), channel_id=1, source_target_pairs={{0,1},{1,2},{2,3},{3,4},{4,5},{5,6},{6,7},{8,9},{9,10},{10,11},{11... | collective-permute-start | bytes 11796488 | tf_op jit(solution)/shard_map/ppermute | solution.py:22
  558.2 71.1 %collective-permute-start.3 = (bf16[2,4,1,1,2,80,1536]{6,5,4,3,1,2,0:T(8,128)(2,1)}, bf16[2,4,1,1,2,80,1536]{6,5,4,3,1,2,0:T(8,128)(2,1)}, u32[]{:S(2)}, u32[]{:S(2)}) collective-permute-start(bf16[2,4,1,1,2,80,1536]{6,5,4,3,1,2,0:T(8,128)(2,1)} %get-tuple-element.154), channel_id=1, source_target_pairs={{1,0},{2,1},{3,2},{4,3},{5,4},{6,5},{7,6},{9,8},{10,9},{11,10},{12... | collective-permute-start | bytes 11796488 | tf_op jit(solution)/shard_map/ppermute | solution.py:24
  566.0 3.3 copy-start.3
  566.0 3.3 copy-start.16
  568.6 60.6 %copy-start.5 = (bf16[1,2,1,2,2,80,1536]{6,5,4,3,1,2,0:T(8,128)(2,1)S(1)}, bf16[1,2,1,2,2,80,1536]{6,5,4,3,1,2,0:T(8,128)(2,1)}, u32[]{:S(2)}) copy-start(bf16[1,2,1,2,2,80,1536]{6,5,4,3,1,2,0:T(8,128)(2,1)} %copy-done.4) | copy-start | bytes 5898244
  568.6 60.6 %copy-start.7 = (bf16[2,1,1,2,2,80,1536]{6,5,4,3,1,2,0:T(8,128)(2,1)S(1)}, bf16[2,1,1,2,2,80,1536]{6,5,4,3,1,2,0:T(8,128)(2,1)}, u32[]{:S(2)}) copy-start(bf16[2,1,1,2,2,80,1536]{6,5,4,3,1,2,0:T(8,128)(2,1)} %copy-done.6) | copy-start | bytes 5898244
  568.6 60.6 %copy-start.9 = (bf16[2,1,1,2,2,80,1536]{6,5,4,3,1,2,0:T(8,128)(2,1)S(1)}, bf16[2,1,1,2,2,80,1536]{6,5,4,3,1,2,0:T(8,128)(2,1)}, u32[]{:S(2)}) copy-start(bf16[2,1,1,2,2,80,1536]{6,5,4,3,1,2,0:T(8,128)(2,1)} %copy-done.8) | copy-start | bytes 5898244
  680.8 9.3 %copy-start.10 = (bf16[12,640,128]{2,1,0:T(8,128)(2,1)S(1)}, bf16[12,640,128]{2,1,0:T(8,128)(2,1)}, u32[]{:S(2)}) copy-start(bf16[12,640,128]{2,1,0:T(8,128)(2,1)} %custom-call) | copy-start | bytes 5898244
  680.8 9.3 %copy-start.13 = (s32[12,3]{0,1:T(4,128)S(1)}, s32[12,3]{0,1:T(4,128)}, u32[]{:S(2)}) copy-start(s32[12,3]{0,1:T(4,128)} %param.16) | copy-start | bytes 436
  832.4 1.3 copy-start.11
  833.7 5.5 copy-start.1
